TPU v7x, 256 devices: a whole 4x4x8 slice. The times are simulated.
256 devices in a mesh: ifg: 64 (over x, z, core), grp: 4 (over y).
Axes of the slice: x: 4, y: 4, z: 8, core: 2. Of those that a mesh axis runs over, the one named last changes fastest.
Arguments:
- phases: bfloat16 [1024, 4, 262144], P('ifg', 'grp'), may hold values from -6 to 6
- date_pairs: int32 [2, 1024], replicated, may hold values from 0 to 199, as said below
- pair_counts: int32 [16], replicated, may hold values from 128 to 1024, as said below
- group_ids: int32 [4, 1024], P(None, 'ifg'), may hold values from 0 to 15, as said below
Outputs:
- series: float32 [4, 200, 262144], P('grp', None, 'ifg')
Inputs may be any that keep to these rules, and one draw needn't show every extreme that they name: date_pairs[0, k] < date_pairs[1, k]; the baseline date_pairs[1, k] - date_pairs[0, k] lies in 1 to 25 and never falls as k grows. `pair_counts`: each count is 128 times a power of two; some class has all 1024 interferograms and some has 128. `group_ids`: constant over each aligned run of 8 blocks of a sub-strip.
All inputs are finite; a program needn't handle non-finite values.
Results may differ from a plain program's by a relative error of at most 0.0003.
Values may be sent and summed in bfloat16 or wider, within the bound.
A program may use at most 128 MiB of HBM per device.

v0:
```python
import jax
import jax.numpy as jnp
from jax import lax
from jax.sharding import PartitionSpec as P

M = 200
BLOCK = 256


damping = 1.0


def solve_blocks(blocks, block_groups, pair_counts, design, inverse):
    total_pairs = blocks.shape[0]
    block_count = blocks.shape[1]
    block_pixels = blocks.shape[2]
    dates_total = design.shape[1]
    class_count = inverse.shape[0]
    class_hot = (block_groups[:, None] == jnp.arange(class_count, dtype=jnp.int32)[None, :]).astype(
        jnp.int32
    )
    block_limit = jnp.sum(class_hot * pair_counts[None, :], axis=1)
    row_index = jnp.arange(total_pairs, dtype=jnp.int32)
    keep_rows = row_index[:, None] < block_limit[None, :]
    masked = jnp.where(keep_rows[:, :, None], blocks, jnp.zeros((), jnp.bfloat16))
    right_side = lax.dot_general(
        design,
        masked.reshape(total_pairs, block_count * block_pixels),
        (((0,), (0,)), ((), ())),
        preferred_element_type=jnp.float32,
    )
    right_side = right_side.reshape(dates_total, block_count, block_pixels)
    block_inverse = jnp.einsum(
        "bg,gmn->bmn", class_hot.astype(jnp.float32), inverse, precision=lax.Precision.HIGHEST
    )
    series = jnp.einsum("bmn,nbp->mbp", block_inverse, right_side, precision=lax.Precision.HIGHEST)
    return series.reshape(dates_total, block_count * block_pixels)


def local(phases, date_pairs, pair_counts, group_ids):
    owner_count = lax.axis_size("ifg")
    total_pairs = date_pairs.shape[1]
    date_index = jnp.arange(M, dtype=jnp.int32)
    design = (
        (date_index[None, :] == date_pairs[1][:, None]).astype(jnp.float32)
        - (date_index[None, :] == date_pairs[0][:, None]).astype(jnp.float32)
    ).astype(jnp.bfloat16)
    identity = jnp.eye(M, dtype=jnp.float32)
    slab_rows = total_pairs // 8
    design_slabs = design.reshape(8, slab_rows, M)
    slab_grams = jnp.einsum(
        "skm,skn->smn", design_slabs, design_slabs, preferred_element_type=jnp.float32
    )
    take_slab = (
        jnp.arange(8, dtype=jnp.int32)[None, :] < (pair_counts // slab_rows)[:, None]
    ).astype(jnp.float32)
    gram_sums = jnp.einsum("gs,smn->gmn", take_slab, slab_grams, precision=lax.Precision.HIGHEST)
    gram_sums = gram_sums + damping * identity
    factors = jnp.linalg.cholesky(gram_sums)
    lower_inverse = jax.scipy.linalg.solve_triangular(
        factors, jnp.broadcast_to(identity, gram_sums.shape), lower=True
    )
    inverse = jnp.einsum(
        "gkm,gkn->gmn", lower_inverse, lower_inverse, precision=lax.Precision.HIGHEST
    )
    strip_index = lax.axis_index("grp")
    local_pairs = phases.shape[0]
    owner_pixels = phases.shape[2] // owner_count
    block_count = owner_pixels // BLOCK
    outgoing = phases.reshape(local_pairs, owner_count, owner_pixels)
    received = lax.all_to_all(outgoing, "ifg", split_axis=1, concat_axis=0, tiled=True)
    blocks = received.reshape(total_pairs, block_count, BLOCK)
    block_groups = lax.dynamic_index_in_dim(group_ids, strip_index, 0, keepdims=False)
    solved = solve_blocks(blocks, block_groups, pair_counts, design, inverse)
    return solved[None, :, :]


def solution(mesh):
    in_specs = (P("ifg", "grp", None), P(), P(), P(None, "ifg"))
    out_specs = P("grp", None, "ifg")
    return jax.shard_map(local, mesh=mesh, in_specs=in_specs, out_specs=out_specs, check_vma=False)
```

profile of v0, /device:TPU:1, one launch (start us, length us, event | category | flops | bytes accessed | tf_op | source)
XLA Modules:
  0.0 900.1 jit_solution(16180793502543684412)
XLA Ops:
  0.0 11.2 %copy.70 = bf16[2,8,64,4096]{3,2,1,0:T(8,128)(2,1)} copy(bf16[2,8,64,4096]{3,1,2,0:T(8,128)(2,1)} %bitcast.67) | data formatting | bytes 16777216
  11.2 11.2 %copy.48 = bf16[16,64,4096]{2,0,1:T(8,128)(2,1)} copy(bf16[16,64,4096]{2,1,0:T(8,128)(2,1)} %bitcast.64) | data formatting | bytes 16777216 | tf_op jit(solution)/shard_map/reshape | solution.py:70
  22.4 13.7 %all-to-all-start = ((bf16[16,64,4096]{2,0,1:T(8,128)(2,1)}), bf16[16,64,4096]{2,0,1:T(8,128)(2,1)}, u32[]{:S(2)}, u32[]{:S(2)}) async-start(bf16[16,64,4096]{2,0,1:T(8,128)(2,1)} %copy.48), calls=%async_computation | async-start | bytes 16777216 | tf_op jit(solution)/shard_map/all_to_all | solution.py:71
  38.4 6.9 broadcast_in_dim.18
  45.4 6.2 copy.69
  52.1 1.7 fusion.13
  53.8 3.2 copy.52
  57.0 4.3 fusion.5
  63.1 188.7 %custom-call.17 = f32[16,128,128]{2,1,0:T(8,128)} custom-call(f32[16,128,128]{2,1,0:T(8,128)S(1)} %cholesky.129), custom_call_target="Cholesky" | custom-call | tf_op jit(solution)/shard_map/jit(cholesky)/cholesky | solution.py:59
  254.5 158.6 %custom-call.18 = f32[16,1,128,128]{2,3,1,0:T(8,128)} custom-call(f32[16,1,128,128]{3,2,1,0:T(8,128)} %get-tuple-element.26), custom_call_target="InvertDiagBlocksLowerTriangular" | custom-call | tf_op jit(solution)/shard_map/jit(cholesky)/cholesky | solution.py:59
  413.1 2.5 constant_dynamic-update-slice_fusion.1
  415.7 3.0 convolution_subtract_fusion.1
  418.6 107.0 %custom-call.19 = f32[16,72,72]{2,1,0:T(8,128)} custom-call(f32[16,72,72]{2,1,0:T(8,128)} %convolution_subtract_fusion.1), custom_call_target="Cholesky" | custom-call | tf_op jit(solution)/shard_map/jit(cholesky)/cholesky | solution.py:59
  529.5 315.2 %custom-call.20 = f32[16,2,128,128]{2,3,1,0:T(8,128)} custom-call(f32[16,2,128,128]{3,2,1,0:T(8,128)S(1)} %pad_maximum_fusion), custom_call_target="InvertDiagBlocksLowerTriangular" | custom-call | tf_op jit(solution)/shard_map/jit(_solve_triangular)/vmap()/triangular_solve | solution.py:60
  844.8 3.9 fusion.15
  848.8 4.3 convolution_subtract_fusion
  853.1 3.9 fusion.21
  857.0 3.4 fusion
  860.4 3.8 fusion.8
  864.2 8.7 bitcast_select_fusion
  872.9 12.0 %copy.68 = bf16[4096,1024]{1,0:T(8,128)(2,1)} copy(bf16[4096,1024]{0,1:T(8,128)(2,1)} %bitcast.63) | data formatting | bytes 16777216 | tf_op jit(solution)/shard_map/dot_general | solution.py:26
  884.9 6.2 fusion.24
  891.1 5.3 fusion.10
  897.5 2.3 broadcast_in_dim_reshape.3
  (48 shorter events, 12.2 us)
Async XLA Ops:
  0.0 38.1 %copy-start = (s32[4,16]{1,0:T(4,128)S(1)}, s32[4,16]{1,0:T(4,128)}, u32[]{:S(2)}) copy-start(s32[4,16]{1,0:T(4,128)} %param.7) | copy-start | bytes 772
  22.4 15.7 %copy-start.8 = (s32[16]{0:T(128)S(1)}, s32[16]{0:T(128)}, u32[]{:S(2)}) copy-start(s32[16]{0:T(128)} %param.6) | copy-start | bytes 196
  22.4 841.8 %all-to-all-start = ((bf16[16,64,4096]{2,0,1:T(8,128)(2,1)}), bf16[16,64,4096]{2,0,1:T(8,128)(2,1)}, u32[]{:S(2)}, u32[]{:S(2)}) async-start(bf16[16,64,4096]{2,0,1:T(8,128)(2,1)} %copy.48), calls=%async_computation | async-start | bytes 16777216 | tf_op jit(solution)/shard_map/all_to_all | solution.py:71
  45.3 6.2 copy-start.7
  61.3 1.7 copy-start.2
  251.8 1.6 copy-start.4
  527.5 1.7 copy-start.3
  528.1 316.6 %copy-start.5 = (f32[128,200]{1,0:T(8,128)S(1)}, f32[128,200]{1,0:T(8,128)}, u32[]{:S(2)}) copy-start(f32[128,200]{1,0:T(8,128)} %triangular_solve.112) | copy-start | bytes 307204
  529.3 319.5 %copy-start.6 = (f32[72,200]{1,0:T(8,128)S(1)}, f32[72,200]{1,0:T(8,128)}, u32[]{:S(2)}) copy-start(f32[72,200]{1,0:T(8,128)} %triangular_solve.114) | copy-start | bytes 172804
  896.4 3.4 copy-start.1
where the time goes:
time: 909 us; the launch traced here: 900 us
  other arithmetic  787 us (87%)
  local copies, waits for them, and re-layouts  60.2 us (7%)
  matrix products  38.5 us (4%)
  starting transfers between devices  13.7 us (2%)
    another operation x10, other arithmetic, local(): factors = jnp.linalg.cholesky(gram_sums)  457 us
    another operation x7, other arithmetic, local(): jax.scipy.linalg.solve_triangular(factors, jnp.broadcast_to(identity, gra...  316 us
    unnamed x20, local copies, waits for them, and re-layouts  20.2 us
  transfers between devices with their start and end apart: 1, of which 0 were waited for; matrix products, arithmetic and copies ran while one was open for 92% of the time, Pallas kernels for 0%

commit v1 on v0

v1 whole, which is shorter than its diff:
```python
import jax
import jax.numpy as jnp
from jax import lax
from jax.experimental import pallas as pl
from jax.experimental.pallas import tpu as pltpu
from jax.sharding import PartitionSpec as P

M = 200
MP = 208
PIX = 4096
HALF = 2048
CPX = 512
NC = PIX // CPX
LOOK = 4
LAG = 1
MESH = pl.DeviceIdType.MESH
OWN_BLOCK = (0, 0, 0)
LEFT = ((0, -1, 128), (-1, -2, 256), (-2, -3, 384))
RIGHT = ((0, 1, 640), (1, 2, 768), (2, 3, 896))
FAR = ((-3, -4, 512), (3, 4, 512))


def split3(value):
    high = value.astype(jnp.bfloat16)
    rest = value - high.astype(jnp.float32)
    middle = rest.astype(jnp.bfloat16)
    low = (rest - middle.astype(jnp.float32)).astype(jnp.bfloat16)
    return high, middle, low


def body(
    src, dates, hot, out,
    land, inverse, design, near_hot, w_own, w_left, w_right, sums_out, sums_in, scale_out, scale_in,
    raw_send, raw_recv, hot_send, hot_recv, sum_send, sum_recv, scale_send, scale_recv,
):
    me = lax.axis_index("ifg")
    core = lax.rem(me, 2)
    z = lax.rem(lax.div(me, 2), 8)
    x = lax.div(me, 16)

    def device(x_at, z_at, core_at):
        return lax.rem(x_at, 4) * 16 + lax.rem(z_at + 16, 8) * 2 + lax.rem(core_at, 2)

    left, right = device(x, z - 1, core), device(x, z + 1, core)

    barrier = pltpu.get_barrier_semaphore()

    def greet(step, carry):
        peer = device(x + lax.div(step, 2), z, core + lax.rem(step, 2))
        for offset in (-3, -2, -1, 1, 2, 3):
            there = device(x + lax.div(step, 2), z + offset, core + lax.rem(step, 2))
            pl.semaphore_signal(barrier, inc=1, device_id={"ifg": there}, device_id_type=MESH)

        @pl.when(step > 0)
        def _():
            pl.semaphore_signal(barrier, inc=1, device_id={"ifg": peer}, device_id_type=MESH)

        return carry

    lax.fori_loop(0, 8, greet, 0)
    pl.semaphore_wait(barrier, 55)

    hot_copies = []
    for side, there in ((0, right), (1, left)):
        copy = pltpu.make_async_remote_copy(
            src_ref=hot, dst_ref=near_hot.at[side], send_sem=hot_send.at[side], recv_sem=hot_recv.at[side],
            device_id={"ifg": there}, device_id_type=MESH,
        )
        copy.start()
        hot_copies.append(copy)

    my_rows = x * 32 + core * 16

    def raw_parts(block, chunk, x_at, core_at):
        helper, owner, first = block
        there = device(x_at, z + helper, core_at)
        owner_index = device(x_at, z + owner, core_at)
        columns = pl.ds(pl.multiple_of(owner_index * PIX + chunk * CPX, 128), CPX)
        rows = pl.ds(pl.multiple_of(first + my_rows, 16), 16)
        landing = pl.ds(pl.multiple_of(chunk * CPX, 128), CPX)
        return src.at[:, columns], land.at[rows, landing], there

    def raw_blocks(half):
        near = [OWN_BLOCK, LEFT[0], RIGHT[0]]
        far = [FAR[half], LEFT[2], RIGHT[2], LEFT[1], RIGHT[1]]
        return near, far

    def send_raw(chunk, half):
        near, far = raw_blocks(half)

        def remote(block, x_at, core_at):
            source, target, there = raw_parts(block, chunk, x_at, core_at)
            pltpu.make_async_remote_copy(
                src_ref=source, dst_ref=target, send_sem=raw_send.at[chunk], recv_sem=raw_recv.at[chunk],
                device_id={"ifg": there}, device_id_type=MESH,
            ).start()

        for block in far:
            remote(block, x, core)

        def peer(step, carry):
            for block in far + near:
                remote(block, x + lax.div(step, 2), core + lax.rem(step, 2))
            return carry

        lax.fori_loop(1, 8, peer, 0)
        for block in near:
            source, target, _ = raw_parts(block, chunk, x, core)
            pltpu.make_async_copy(source, target, raw_recv.at[chunk]).start()

    def wait_raw(chunk, sem, rows):
        view = land.at[pl.ds(0, rows), pl.ds(pl.multiple_of(chunk * CPX, 128), CPX)]
        pltpu.make_async_copy(view, view, sem.at[chunk]).wait()

    for chunk in range(LOOK):
        send_raw(chunk, chunk // (NC // 2))

    date_at = lax.broadcasted_iota(jnp.int32, (256, 1024), 0)
    signs = (date_at == dates[1:2, :]).astype(jnp.float32) - (date_at == dates[0:1, :]).astype(jnp.float32)
    design[...] = signs.astype(jnp.bfloat16)
    place = lax.broadcasted_iota(jnp.int32, (1, 1024), 1)
    pair = ((place >> 5) & 3) * 256 + (place >> 7) * 32 + (place & 31)
    eye = (
        lax.broadcasted_iota(jnp.int32, (MP, 256), 0) == lax.broadcasted_iota(jnp.int32, (MP, 256), 1)
    ).astype(jnp.float32)
    keep = [(pair < (128 << level)).astype(jnp.float32) for level in range(4)]
    for level in range(4):
        gram = lax.dot_general(
            design[0:MP, :], (signs * keep[level]).astype(jnp.bfloat16), (((1,), (1,)), ((), ())),
            preferred_element_type=jnp.float32,
        )
        inverse[level] = gram + eye
    lane = lax.broadcasted_iota(jnp.int32, (1, 1, 256), 2)
    lane_half = lax.broadcasted_iota(jnp.int32, (1, 1, 128), 2)

    def eliminate(side):
        mine, other = slice(side * 128, side * 128 + 128), slice(128 - side * 128, 256 - side * 128)

        def step(index, carry):
            hit = lane_half == index - side * 128
            row = inverse[:, pl.ds(index, 1), :]
            block = inverse[:, :, mine]
            column = jnp.sum(jnp.where(hit, block, 0.0), axis=2, keepdims=True)
            pivot = 1.0 / jnp.sum(jnp.where(hit, row[:, :, mine], 0.0), axis=2, keepdims=True)
            scaled = jnp.where(lane == index, pivot, row * pivot)
            inverse[:, :, mine] = jnp.where(hit, 0.0, block) - column * scaled[:, :, mine]
            inverse[:, :, other] = inverse[:, :, other] - column * scaled[:, :, other]
            inverse[:, pl.ds(index, 1), :] = scaled
            return carry

        return step

    lax.fori_loop(0, 128, eliminate(0), 0)
    lax.fori_loop(128, M, eliminate(1), 0)

    for copy in hot_copies:
        copy.wait()

    def weights(flags, run, blocks, target):
        flag = [flags[2 * level + run : 2 * level + run + 1, 0:1] for level in range(4)]
        parts = split3(sum(flag[level] * inverse[level] for level in range(4)))
        column = lax.broadcasted_iota(jnp.int32, (1, 128), 1)
        for at, offset in enumerate(blocks):
            z_at = lax.rem(z + offset + 16, 8)
            block = design[:, pl.ds(pl.multiple_of(z_at * 128, 128), 128)]
            value = sum(jnp.dot(part, block, preferred_element_type=jnp.float32) for part in parts)
            pair_at = (column >> 5) * 256 + z_at * 32 + (column & 31)
            value = value * sum(flag[level] * (pair_at < (128 << level)).astype(jnp.float32) for level in range(4))
            high = value.astype(jnp.bfloat16)
            low = (value - high.astype(jnp.float32)).astype(jnp.bfloat16)
            target[run, 0:MP, at * 128 : at * 128 + 128] = high
            target[run, MP : 2 * MP, at * 128 : at * 128 + 128] = low

    for run in range(2):
        weights(hot, run, (0,), w_own)
        weights(near_hot.at[0], run, (0, 1, 2, 3)[: 4 - run], w_left)
        weights(near_hot.at[1], run, (0, -1, -2) if run == 0 else (-3, 0, -1, -2), w_right)

    def apply(weight, chunk, first, depth):
        data = land[first : first + depth, pl.ds(pl.multiple_of(chunk * CPX, 128), CPX)]
        both = jnp.dot(weight, data, preferred_element_type=jnp.float32)
        return both[0:MP] + both[MP : 2 * MP]

    def sum_copies(chunk):
        copies = []
        for side, there in ((0, left), (1, right)):
            copies.append(pltpu.make_async_remote_copy(
                src_ref=sums_out.at[side, chunk], dst_ref=sums_in.at[side, chunk],
                send_sem=sum_send.at[side, chunk], recv_sem=sum_recv.at[side, chunk],
                device_id={"ifg": there}, device_id_type=MESH,
            ))
            copies.append(pltpu.make_async_remote_copy(
                src_ref=scale_out.at[side, chunk], dst_ref=scale_in.at[side, chunk],
                send_sem=scale_send.at[side, chunk], recv_sem=scale_recv.at[side, chunk],
                device_id={"ifg": there}, device_id_type=MESH,
            ))
        return copies

    def pack(value, side, chunk):
        top = jnp.max(jnp.abs(value), axis=0, keepdims=True)
        factor = 32766.0 / jnp.maximum(top, 1e-30)
        rounded = jnp.round(value * factor).astype(jnp.int32).astype(jnp.int16)
        sums_out[side, chunk] = rounded
        unit = top * (1.0 / 32766.0)
        for piece in range(CPX // 128):
            scale_out[side, chunk, piece : piece + 1, :] = unit[:, piece * 128 : piece * 128 + 128]

    def finish(chunk):
        for copy in sum_copies(chunk):
            copy.wait_recv()
        columns = pl.ds(pl.multiple_of(chunk * CPX, 128), CPX)
        total = out[:, columns]
        for side in range(2):
            unit = jnp.concatenate(
                [scale_in[side, chunk, piece : piece + 1, :] for piece in range(CPX // 128)], axis=1
            )
            total = total + sums_in[side, chunk, 0:M, :].astype(jnp.int32).astype(jnp.float32) * unit
        out[:, columns] = total

    def work(half):
        left_rows = (128, 512 if half == 0 else 384)
        right_rows = (640, 384) if half == 0 else (512, 512)

        def step(chunk, carry):
            wait_raw(chunk, raw_recv, 1024)
            if half == 0:
                ahead = chunk + LOOK
                @pl.when(ahead < NC)
                def _():
                    send_raw(ahead, 1)
            pack(apply(w_left[half, :, 0 : left_rows[1]], chunk, *left_rows), 0, chunk)
            pack(apply(w_right[half, :, 0 : right_rows[1]], chunk, *right_rows), 1, chunk)
            out[:, pl.ds(pl.multiple_of(chunk * CPX, 128), CPX)] = apply(w_own[half], chunk, 0, 128)[0:M]
            for copy in sum_copies(chunk):
                copy.start()

            @pl.when(chunk >= LAG)
            def _():
                finish(chunk - LAG)

            return carry

        return step

    lax.fori_loop(0, NC // 2, work(0), 0)
    lax.fori_loop(NC // 2, NC, work(1), 0)
    for chunk in range(NC - LAG, NC):
        finish(chunk)

    def drain(chunk, carry):
        wait_raw(chunk, raw_send, 976)
        for copy in sum_copies(chunk):
            copy.wait_send()
        return carry

    lax.fori_loop(0, NC, drain, 0)


def local(phases, date_pairs, pair_counts, group_ids):
    rows = phases.shape[0]
    source = phases.reshape(rows, phases.shape[2])
    dates = date_pairs.reshape(2, 4, 8, 32).transpose(0, 2, 1, 3).reshape(2, 1024)
    groups = lax.dynamic_index_in_dim(group_ids, lax.axis_index("grp"), 0, keepdims=False)
    run_groups = groups.reshape(2, 8)[:, 0]
    picked = run_groups[:, None] == jnp.arange(16, dtype=jnp.int32)[None, :]
    counts = jnp.sum(jnp.where(picked, pair_counts[None, :], 0), axis=1)
    levels = jnp.array([128, 256, 512, 1024], jnp.int32)
    hot = (levels[:, None] == counts[None, :]).astype(jnp.float32).reshape(8, 1)
    hot = jnp.broadcast_to(hot, (8, 128))
    vmem = pl.BlockSpec(memory_space=pltpu.VMEM)
    solved = pl.pallas_call(
        body,
        out_shape=jax.ShapeDtypeStruct((M, PIX), jnp.float32),
        in_specs=[pl.BlockSpec(memory_space=pl.ANY), vmem, vmem],
        out_specs=vmem,
        scratch_shapes=[
            pltpu.VMEM((1024, PIX), jnp.bfloat16),
            pltpu.VMEM((4, MP, 256), jnp.float32),
            pltpu.VMEM((256, 1024), jnp.bfloat16),
            pltpu.VMEM((2, 8, 128), jnp.float32),
            pltpu.VMEM((2, 2 * MP, 128), jnp.bfloat16),
            pltpu.VMEM((2, 2 * MP, 512), jnp.bfloat16),
            pltpu.VMEM((2, 2 * MP, 512), jnp.bfloat16),
            pltpu.VMEM((2, NC, MP, CPX), jnp.int16),
            pltpu.VMEM((2, NC, MP, CPX), jnp.int16),
            pltpu.VMEM((2, NC, 8, 128), jnp.float32),
            pltpu.VMEM((2, NC, 8, 128), jnp.float32),
            pltpu.SemaphoreType.DMA((NC,)),
            pltpu.SemaphoreType.DMA((NC,)),
            pltpu.SemaphoreType.DMA((2,)),
            pltpu.SemaphoreType.DMA((2,)),
            pltpu.SemaphoreType.DMA((2, NC)),
            pltpu.SemaphoreType.DMA((2, NC)),
            pltpu.SemaphoreType.DMA((2, NC)),
            pltpu.SemaphoreType.DMA((2, NC)),
        ],
        compiler_params=pltpu.CompilerParams(
            collective_id=0, has_side_effects=True, vmem_limit_bytes=60 * 1024 * 1024
        ),
    )(source, dates, hot)
    return solved[None, :, :]


def solution(mesh):
    in_specs = (P("ifg", "grp", None), P(), P(), P(None, "ifg"))
    out_specs = P("grp", None, "ifg")
    return jax.shard_map(local, mesh=mesh, in_specs=in_specs, out_specs=out_specs, check_vma=False)
```

time: 909 us -> 183 us (0.20)
  other arithmetic: 787 us -> 1.56 us
  Pallas kernels: 0 us -> 174 us
  local copies, waits for them, and re-layouts: 60.2 us -> 7.09 us
  matrix products: 38.5 us -> 0 us
  starting transfers between devices: 13.7 us -> 0 us
    another operation x17 -> x0, other arithmetic: 773 us -> none  [the longest x10 457 us: local(): factors = jnp.linalg.cholesky(gram_sums)]
    pallas_call x0 -> x1, Pallas kernels: none -> 174 us  [local(): pl.pallas_call(body, out_shape=jax.ShapeDtypeStruct((M, PIX), jnp.float32...]
    dot_general x6 -> x0, matrix products: 20.9 us -> none  [the longest x1 6.17 us: solve_blocks(): lax.dot_general(design, masked.reshape(total_pairs, block_count * block_p...]
    another operation x5 -> x0, matrix products: 17.6 us -> none  [the longest x3 12.1 us: local(): jax.scipy.linalg.solve_triangular(factors, jnp.broadcast_to(identity, gra...]
    unnamed x20 -> x3, local copies, waits for them, and re-layouts: 20.2 us -> 4.64 us
    dot_general x2 -> x0, local copies, waits for them, and re-layouts: 15.1 us -> none  [the longest x1 12 us: solve_blocks(): lax.dot_general(design, masked.reshape(total_pairs, block_count * block_p...]
    all_to_all x1 -> x0, starting transfers between devices: 13.7 us -> none  [local(): lax.all_to_all(outgoing, 'ifg', split_axis=1, concat_axis=0, tiled=True)]
    reshape x1 -> x4, local copies, waits for them, and re-layouts: 11.2 us -> 1.56 us  [the longest x3 1.48 us: local(): date_pairs.reshape(2, 4, 8, 32).transpose(0, 2, 1, 3).reshape(2, 1024)]
  transfers between devices with their start and end apart: 1 -> 0, of which waited for: 0 -> 0; matrix products, arithmetic and copies ran while one was open for 92% -> 0% of each run, Pallas kernels for 0% -> 0%
where the time goes in v1:
time: 183 us
  Pallas kernels  174 us (95%)
  local copies, waits for them, and re-layouts  7.09 us (4%)
    pallas_call x1, Pallas kernels, local(): pl.pallas_call(body, out_shape=jax.ShapeDtypeStruct((M, PIX), jnp.float32...  174 us
    unnamed x3, local copies, waits for them, and re-layouts  4.64 us

profile of v1, /device:TPU:1, one launch (start us, length us, event | category | flops | bytes accessed | tf_op | source)
XLA Modules:
  0.0 182.5 jit_solution(13986358711795991784)
XLA Ops:
  0.0 0.0 copy-start
  0.0 0.7 copy-done
  0.7 0.1 reshape.37
  0.8 0.1 slice_reduce_fusion
  0.9 0.8 fusion
  1.7 0.7 compare_convert_fusion
  2.5 0.1 reshape.38
  2.6 0.7 broadcast_in_dim.26.hot
  3.2 0.8 reshape.35
  4.0 0.7 reshape.36.dates
  4.7 173.8 %shard_map.55 = f32[200,4096]{1,0:T(8,128)} custom-call(bf16[16,262144]{1,0:T(8,128)(2,1)} %bitcast.6, s32[2,1024]{1,0:T(2,128)} %reshape.36.dates, f32[8,128]{1,0:T(8,128)} %broadcast_in_dim.26.hot), custom_call_target="tpu_custom_call" | custom-call | tf_op jit(solution)/shard_map/pallas_call | solution.py:271
  178.5 4.0 %copy.12 = f32[1,200,4096]{2,1,0:T(8,128)} copy(f32[1,200,4096]{2,1,0:T(8,128)} %bitcast.5) | data formatting | bytes 6553600
  (2 shorter events, 0.0 us)
Async XLA Ops:
  0.0 0.7 copy-start

commit v2 on v1

v2 whole, which is shorter than its diff:
```python
import jax
import jax.numpy as jnp
from jax import lax
from jax.experimental import pallas as pl
from jax.experimental.pallas import tpu as pltpu
from jax.sharding import PartitionSpec as P

M = 200
MP = 208
PIX = 4096
CPX = 512
NC = PIX // CPX
LOOK = NC
LAG = 1
EDGE = 88
SEAM = 113
GAP = 128 - SEAM
MESH = pl.DeviceIdType.MESH
SAME = ((0, 0, 0), (0, -1, 128), (0, 1, 256), (0, -2, 384), (0, 2, 768))
NEXT = ((-1, -3, 512), (1, 3, 896))
FAR = ((-2, -4, 640), (2, 4, 640))


def split3(value):
    high = value.astype(jnp.bfloat16)
    rest = value - high.astype(jnp.float32)
    middle = rest.astype(jnp.bfloat16)
    low = (rest - middle.astype(jnp.float32)).astype(jnp.bfloat16)
    return high, middle, low


def body(
    src, dates, hot, out,
    land, halves, inverse, design, near_hot, w_own, w_near, w_left, w_right,
    sums_out, sums_in, scale_out, scale_in,
    raw_send, raw_recv, hot_send, hot_recv, sum_send, sum_recv, scale_send, scale_recv,
):
    me = lax.axis_index("ifg")
    core = lax.rem(me, 2)
    z = lax.rem(lax.div(me, 2), 8)
    x = lax.div(me, 16)

    def device(x_at, z_at, core_at):
        return lax.rem(x_at, 4) * 16 + lax.rem(z_at + 16, 8) * 2 + lax.rem(core_at, 2)

    left, right = device(x, z - 1, core), device(x, z + 1, core)

    barrier = pltpu.get_barrier_semaphore()

    def greet(step, carry):
        peer = device(x + lax.div(step, 2), z, core + lax.rem(step, 2))
        for offset in (-2, -1, 1, 2):
            there = device(x + lax.div(step, 2), z + offset, core + lax.rem(step, 2))
            pl.semaphore_signal(barrier, inc=1, device_id={"ifg": there}, device_id_type=MESH)

        @pl.when(step > 0)
        def _():
            pl.semaphore_signal(barrier, inc=1, device_id={"ifg": peer}, device_id_type=MESH)

        return carry

    lax.fori_loop(0, 8, greet, 0)
    pl.semaphore_wait(barrier, 39)

    hot_copies = []
    for slot, offset in enumerate((1, -1, 2, -2)):
        copy = pltpu.make_async_remote_copy(
            src_ref=hot, dst_ref=near_hot.at[slot], send_sem=hot_send.at[slot], recv_sem=hot_recv.at[slot],
            device_id={"ifg": device(x, z + offset, core)}, device_id_type=MESH,
        )
        copy.start()
        hot_copies.append(copy)

    my_rows = x * 32 + core * 16

    def raw_parts(block, chunk, x_at, core_at):
        helper, owner, first = block
        there = device(x_at, z + helper, core_at)
        owner_index = device(x_at, z + owner, core_at)
        columns = pl.ds(pl.multiple_of(owner_index * PIX + chunk * CPX, 128), CPX)
        rows = pl.ds(pl.multiple_of(first + my_rows, 16), 16)
        landing = pl.ds(pl.multiple_of(chunk * CPX, 128), CPX)
        return src.at[:, columns], land.at[rows, landing], there

    def send_raw(chunk, half):
        away = (FAR[half],) + NEXT

        def remote(block, x_at, core_at):
            source, target, there = raw_parts(block, chunk, x_at, core_at)
            pltpu.make_async_remote_copy(
                src_ref=source, dst_ref=target, send_sem=raw_send.at[chunk], recv_sem=raw_recv.at[chunk],
                device_id={"ifg": there}, device_id_type=MESH,
            ).start()

        for block in away:
            remote(block, x, core)

        def peer(step, carry):
            for block in away + SAME:
                remote(block, x + lax.div(step, 2), core + lax.rem(step, 2))
            return carry

        lax.fori_loop(1, 8, peer, 0)
        for block in SAME:
            source, target, _ = raw_parts(block, chunk, x, core)
            pltpu.make_async_copy(source, target, raw_recv.at[chunk]).start()

    def wait_raw(chunk, sem, rows):
        view = land.at[pl.ds(0, rows), pl.ds(pl.multiple_of(chunk * CPX, 128), CPX)]
        pltpu.make_async_copy(view, view, sem.at[chunk]).wait()

    for chunk in range(LOOK):
        send_raw(chunk, chunk // (NC // 2))

    date_at = lax.broadcasted_iota(jnp.int32, (256, 1024), 0)
    placed = jnp.where(dates[...] < SEAM, dates[...], dates[...] + GAP)
    signs = (date_at == placed[1:2, :]).astype(jnp.float32) - (date_at == placed[0:1, :]).astype(jnp.float32)
    design[...] = signs.astype(jnp.bfloat16)
    place = lax.broadcasted_iota(jnp.int32, (1, 1024), 1)
    pair = ((place >> 5) & 3) * 256 + (place >> 7) * 32 + (place & 31)
    down = lax.broadcasted_iota(jnp.int32, (128, 128), 0)
    across = lax.broadcasted_iota(jnp.int32, (128, 128), 1)
    eye = (down == across).astype(jnp.float32)
    for level in range(4):
        kept = (signs * (pair < (128 << level)).astype(jnp.float32)).astype(jnp.bfloat16)
        gram = lax.dot_general(
            design[...], kept, (((1,), (1,)), ((), ())), preferred_element_type=jnp.float32
        )
        halves[level] = gram[0:128, 0:128] + eye
        halves[4 + level] = (
            gram[128:256, 128:256] + gram[0:128, 128:256] + gram[128:256, 0:128] + jnp.where(down < EDGE, eye, 0.0)
        )

    def eliminate(work, rows, side, lanes):
        mine = slice(side * 128, side * 128 + 128)
        rest = [slice(at * 128, at * 128 + 128) for at in range(lanes // 128) if at != side]
        lane = lax.broadcasted_iota(jnp.int32, (1, 1, lanes), 2)
        lane_mine = lax.broadcasted_iota(jnp.int32, (1, 1, 128), 2)

        def step(index, carry):
            hit = lane_mine == index - side * 128
            row = work[:, pl.ds(index, 1), :]
            block = work[:, 0:rows, mine]
            column = jnp.sum(jnp.where(hit, block, 0.0), axis=2, keepdims=True)
            pivot = 1.0 / jnp.sum(jnp.where(hit, row[:, :, mine], 0.0), axis=2, keepdims=True)
            scaled = jnp.where(lane == index, pivot, row * pivot)
            work[:, 0:rows, mine] = jnp.where(hit, 0.0, block) - column * scaled[:, :, mine]
            for other in rest:
                work[:, 0:rows, other] = work[:, 0:rows, other] - column * scaled[:, :, other]
            work[:, pl.ds(index, 1), :] = scaled
            return carry

        return step

    lax.fori_loop(0, EDGE, eliminate(halves, 120, 0, 128), 0)
    low_row, low_lane = down < EDGE, across < EDGE
    for level in range(4):
        after = halves[4 + level]
        inverse[level, 0:128, 0:128] = halves[level] + jnp.where(low_row | low_lane, 0.0, after)
        inverse[level, 0:128, 128:256] = jnp.where(low_lane & ~low_row, after, 0.0)
        inverse[level, 128:216, 0:128] = jnp.where(low_row & ~low_lane, after, 0.0)[0:EDGE]
        inverse[level, 128:216, 128:256] = jnp.where(low_row & low_lane, after, 0.0)[0:EDGE]
    lax.fori_loop(EDGE, SEAM, eliminate(inverse, 216, 0, 256), 0)

    for copy in hot_copies:
        copy.wait()

    def weights(flags, run, blocks, target):
        flag = [flags[2 * level + run : 2 * level + run + 1, 0:1] for level in range(4)]
        chosen = sum(flag[level] * inverse[level] for level in range(4))
        chosen = jnp.concatenate([chosen[0:SEAM], chosen[128 : 128 + M - SEAM], jnp.zeros((MP - M, 256), jnp.float32)])
        parts = split3(chosen)
        column = lax.broadcasted_iota(jnp.int32, (1, 128), 1)
        for at, offset in enumerate(blocks):
            z_at = lax.rem(z + offset + 16, 8)
            block = design[:, pl.ds(pl.multiple_of(z_at * 128, 128), 128)]
            value = sum(jnp.dot(part, block, preferred_element_type=jnp.float32) for part in parts)
            pair_at = (column >> 5) * 256 + z_at * 32 + (column & 31)
            value = value * sum(flag[level] * (pair_at < (128 << level)).astype(jnp.float32) for level in range(4))
            high = value.astype(jnp.bfloat16)
            low = (value - high.astype(jnp.float32)).astype(jnp.bfloat16)
            target[0:MP, at * 128 : at * 128 + 128] = high
            target[MP : 2 * MP, at * 128 : at * 128 + 128] = low

    for run in range(2):
        weights(near_hot.at[2], run, (0, 1, 2)[: 3 - run], w_left.at[run])
        weights(near_hot.at[3], run, (0, -1) if run == 0 else (-2, 0, -1), w_right.at[run])
        weights(near_hot.at[0], run, (0,), w_near.at[0, run])
        weights(near_hot.at[1], run, (0,), w_near.at[1, run])
        weights(hot, run, (0,), w_own.at[run])

    def apply(weight, chunk, first, depth):
        data = land[first : first + depth, pl.ds(pl.multiple_of(chunk * CPX, 128), CPX)]
        both = jnp.dot(weight, data, preferred_element_type=jnp.float32)
        return both[0:MP] + both[MP : 2 * MP]

    def sum_copies(stage, chunk):
        copies = []
        for side, there in ((0, left), (1, right)):
            copies.append(pltpu.make_async_remote_copy(
                src_ref=sums_out.at[stage, side, chunk], dst_ref=sums_in.at[stage, side, chunk],
                send_sem=sum_send.at[stage, side, chunk], recv_sem=sum_recv.at[stage, side, chunk],
                device_id={"ifg": there}, device_id_type=MESH,
            ))
            copies.append(pltpu.make_async_remote_copy(
                src_ref=scale_out.at[stage, side, chunk], dst_ref=scale_in.at[stage, side, chunk],
                send_sem=scale_send.at[stage, side, chunk], recv_sem=scale_recv.at[stage, side, chunk],
                device_id={"ifg": there}, device_id_type=MESH,
            ))
        return copies

    def pack(value, stage, side, chunk):
        top = jnp.max(jnp.abs(value), axis=0, keepdims=True)
        factor = 32766.0 / jnp.maximum(top, 1e-30)
        rounded = jnp.round(value * factor).astype(jnp.int32).astype(jnp.int16)
        sums_out[stage, side, chunk] = rounded
        unit = top * (1.0 / 32766.0)
        for piece in range(CPX // 128):
            scale_out[stage, side, chunk, piece : piece + 1, :] = unit[:, piece * 128 : piece * 128 + 128]

    def unpack(stage, side, chunk, rows):
        unit = jnp.concatenate(
            [scale_in[stage, side, chunk, piece : piece + 1, :] for piece in range(CPX // 128)], axis=1
        )
        return sums_in[stage, side, chunk, 0:rows, :].astype(jnp.int32).astype(jnp.float32) * unit

    def relay(chunk, run):
        for copy in sum_copies(0, chunk):
            copy.wait_recv()
        for side in range(2):
            pack(apply(w_near[side, run], chunk, 128 + 128 * side, 128) + unpack(0, side, chunk, MP), 1, side, chunk)
        for copy in sum_copies(1, chunk):
            copy.start()

    def finish(chunk, run):
        columns = pl.ds(pl.multiple_of(chunk * CPX, 128), CPX)
        own = apply(w_own[run], chunk, 0, 128)[0:M]
        for copy in sum_copies(1, chunk):
            copy.wait_recv()
        out[:, columns] = own + unpack(1, 0, chunk, M) + unpack(1, 1, chunk, M)

    half_count = NC // 2

    def work(half):
        left_depth, right_first = (384, 768) if half == 0 else (256, 640)

        def step(chunk, carry):
            wait_raw(chunk, raw_recv, 1024)
            if half == 0:
                ahead = chunk + LOOK

                @pl.when(ahead < NC)
                def _():
                    send_raw(ahead, 1)

            pack(apply(w_left[half, :, 0:left_depth], chunk, 384, left_depth), 0, 0, chunk)
            pack(apply(w_right[half, :, 0 : 1024 - right_first], chunk, right_first, 1024 - right_first), 0, 1, chunk)
            for copy in sum_copies(0, chunk):
                copy.start()

            @pl.when(chunk >= LAG)
            def _():
                relay(chunk - LAG, lax.div(chunk - LAG, half_count))

            @pl.when(chunk >= 2 * LAG)
            def _():
                finish(chunk - 2 * LAG, lax.div(chunk - 2 * LAG, half_count))

            return carry

        return step

    lax.fori_loop(0, half_count, work(0), 0)
    lax.fori_loop(half_count, NC, work(1), 0)
    for chunk in range(NC - LAG, NC):
        relay(chunk, 1)
    for chunk in range(NC - 2 * LAG, NC):
        finish(chunk, 1)

    def drain(chunk, carry):
        wait_raw(chunk, raw_send, 944)
        for copy in sum_copies(0, chunk) + sum_copies(1, chunk):
            copy.wait_send()
        return carry

    lax.fori_loop(0, NC, drain, 0)


def local(phases, date_pairs, pair_counts, group_ids):
    rows = phases.shape[0]
    source = phases.reshape(rows, phases.shape[2])
    dates = date_pairs.reshape(2, 4, 8, 32).transpose(0, 2, 1, 3).reshape(2, 1024)
    groups = lax.dynamic_index_in_dim(group_ids, lax.axis_index("grp"), 0, keepdims=False)
    run_groups = groups.reshape(2, 8)[:, 0]
    picked = run_groups[:, None] == jnp.arange(16, dtype=jnp.int32)[None, :]
    counts = jnp.sum(jnp.where(picked, pair_counts[None, :], 0), axis=1)
    levels = jnp.array([128, 256, 512, 1024], jnp.int32)
    hot = (levels[:, None] == counts[None, :]).astype(jnp.float32).reshape(8, 1)
    hot = jnp.broadcast_to(hot, (8, 128))
    vmem = pl.BlockSpec(memory_space=pltpu.VMEM)
    solved = pl.pallas_call(
        body,
        out_shape=jax.ShapeDtypeStruct((M, PIX), jnp.float32),
        in_specs=[pl.BlockSpec(memory_space=pl.ANY), vmem, vmem],
        out_specs=vmem,
        scratch_shapes=[
            pltpu.VMEM((1024, PIX), jnp.bfloat16),
            pltpu.VMEM((8, 128, 128), jnp.float32),
            pltpu.VMEM((4, 216, 256), jnp.float32),
            pltpu.VMEM((256, 1024), jnp.bfloat16),
            pltpu.VMEM((4, 8, 128), jnp.float32),
            pltpu.VMEM((2, 2 * MP, 128), jnp.bfloat16),
            pltpu.VMEM((2, 2, 2 * MP, 128), jnp.bfloat16),
            pltpu.VMEM((2, 2 * MP, 384), jnp.bfloat16),
            pltpu.VMEM((2, 2 * MP, 384), jnp.bfloat16),
            pltpu.VMEM((2, 2, NC, MP, CPX), jnp.int16),
            pltpu.VMEM((2, 2, NC, MP, CPX), jnp.int16),
            pltpu.VMEM((2, 2, NC, 8, 128), jnp.float32),
            pltpu.VMEM((2, 2, NC, 8, 128), jnp.float32),
            pltpu.SemaphoreType.DMA((NC,)),
            pltpu.SemaphoreType.DMA((NC,)),
            pltpu.SemaphoreType.DMA((4,)),
            pltpu.SemaphoreType.DMA((4,)),
            pltpu.SemaphoreType.DMA((2, 2, NC)),
            pltpu.SemaphoreType.DMA((2, 2, NC)),
            pltpu.SemaphoreType.DMA((2, 2, NC)),
            pltpu.SemaphoreType.DMA((2, 2, NC)),
        ],
        compiler_params=pltpu.CompilerParams(
            collective_id=0, has_side_effects=True, vmem_limit_bytes=60 * 1024 * 1024
        ),
    )(source, dates, hot)
    return solved[None, :, :]


def solution(mesh):
    in_specs = (P("ifg", "grp", None), P(), P(), P(None, "ifg"))
    out_specs = P("grp", None, "ifg")
    return jax.shard_map(local, mesh=mesh, in_specs=in_specs, out_specs=out_specs, check_vma=False)
```

time: 183 us -> 146 us (0.80)
  Pallas kernels: 174 us -> 137 us
    pallas_call x1, Pallas kernels: 174 us -> 137 us  [local(): pl.pallas_call(body, out_shape=jax.ShapeDtypeStruct((M, PIX), jnp.float32...]
where the time goes in v2:
time: 146 us; the launch traced here: 145 us
  Pallas kernels  137 us (94%)
  local copies, waits for them, and re-layouts  7.09 us (5%)
  other arithmetic  1.56 us (1%)
    pallas_call x1, Pallas kernels, local(): pl.pallas_call(body, out_shape=jax.ShapeDtypeStruct((M, PIX), jnp.float32...  137 us
    unnamed x3, local copies, waits for them, and re-layouts  4.64 us

profile of v2, /device:TPU:1, one launch (start us, length us, event | category | flops | bytes accessed | tf_op | source)
XLA Modules:
  0.0 145.3 jit_solution(13392250320249928739)
XLA Ops:
  0.0 0.0 copy-start
  0.0 0.7 copy-done
  0.7 0.1 reshape.37
  0.8 0.1 slice_reduce_fusion
  0.9 0.8 fusion
  1.7 0.7 compare_convert_fusion
  2.5 0.1 reshape.38
  2.6 0.7 broadcast_in_dim.26.hot
  3.2 0.8 reshape.35
  4.0 0.7 reshape.36.dates
  4.7 136.6 %shard_map.55 = f32[200,4096]{1,0:T(8,128)} custom-call(bf16[16,262144]{1,0:T(8,128)(2,1)} %bitcast.6, s32[2,1024]{1,0:T(2,128)} %reshape.36.dates, f32[8,128]{1,0:T(8,128)} %broadcast_in_dim.26.hot), custom_call_target="tpu_custom_call" | custom-call | tf_op jit(solution)/shard_map/pallas_call | solution.py:301
  141.3 4.0 %copy.12 = f32[1,200,4096]{2,1,0:T(8,128)} copy(f32[1,200,4096]{2,1,0:T(8,128)} %bitcast.5) | data formatting | bytes 6553600
  (2 shorter events, 0.0 us)
Async XLA Ops:
  0.0 0.7 copy-start

commit v3 on v2

--- a/solution.py
+++ b/solution.py
@@ -10,7 +10,7 @@
 PIX = 4096
 CPX = 512
 NC = PIX // CPX
-LOOK = NC
+LEAD = 1
 LAG = 1
 EDGE = 88
 SEAM = 113
@@ -30,10 +30,10 @@
 
 
 def body(
-    src, dates, hot, out,
+    src, date_pairs, pair_counts, group_ids, out,
     land, halves, inverse, design, near_hot, w_own, w_near, w_left, w_right,
-    sums_out, sums_in, scale_out, scale_in,
-    raw_send, raw_recv, hot_send, hot_recv, sum_send, sum_recv, scale_send, scale_recv,
+    sums_out, sums_in, scale_out, scale_in, total, hot,
+    raw_send, raw_recv, hot_send, hot_recv, sum_send, sum_recv, scale_send, scale_recv, out_sem,
 ):
     me = lax.axis_index("ifg")
     core = lax.rem(me, 2)
@@ -62,6 +62,59 @@
     lax.fori_loop(0, 8, greet, 0)
     pl.semaphore_wait(barrier, 39)
 
+    my_rows = x * 32 + core * 16
+
+    def raw_parts(block, chunk, x_at, core_at):
+        helper, owner, first = block
+        there = device(x_at, z + helper, core_at)
+        owner_index = device(x_at, z + owner, core_at)
+        columns = pl.ds(pl.multiple_of(owner_index * PIX + chunk * CPX, 128), CPX)
+        rows = pl.ds(pl.multiple_of(first + my_rows, 16), 16)
+        landing = pl.ds(pl.multiple_of(chunk * CPX, 128), CPX)
+        return src.at[:, columns], land.at[rows, landing], there
+
+    def send_one(block, chunk, x_at, core_at):
+        source, target, there = raw_parts(block, chunk, x_at, core_at)
+        pltpu.make_async_remote_copy(
+            src_ref=source, dst_ref=target, send_sem=raw_send.at[chunk], recv_sem=raw_recv.at[chunk],
+            device_id={"ifg": there}, device_id_type=MESH,
+        ).start()
+
+    def send_away(chunk, half):
+        def peer(step, carry):
+            for block in (FAR[half],) + NEXT:
+                send_one(block, chunk, x + lax.div(step, 2), core + lax.rem(step, 2))
+            return carry
+
+        lax.fori_loop(0, 8, peer, 0)
+
+    def send_same(chunk):
+        def peer(step, carry):
+            for block in SAME:
+                send_one(block, chunk, x + lax.div(step, 2), core + lax.rem(step, 2))
+            return carry
+
+        lax.fori_loop(1, 8, peer, 0)
+        for block in SAME:
+            source, target, _ = raw_parts(block, chunk, x, core)
+            pltpu.make_async_copy(source, target, raw_recv.at[chunk]).start()
+
+    def wait_raw(chunk, sem, rows):
+        view = land.at[pl.ds(0, rows), pl.ds(pl.multiple_of(chunk * CPX, 128), CPX)]
+        pltpu.make_async_copy(view, view, sem.at[chunk]).wait()
+
+    for chunk in range(NC + LEAD):
+        if chunk < NC:
+            send_away(chunk, chunk // (NC // 2))
+        if chunk >= LEAD:
+            send_same(chunk - LEAD)
+
+    groups = group_ids[pl.ds(lax.axis_index("grp"), 1), :]
+    counts = sum(jnp.where(groups == group, pair_counts[group], 0) for group in range(16))
+    for level in range(4):
+        for run in range(2):
+            flag = (counts[:, 8 * run : 8 * run + 1] == (128 << level)).astype(jnp.float32)
+            hot[2 * level + run : 2 * level + run + 1, :] = jnp.broadcast_to(flag, (1, 128))
     hot_copies = []
     for slot, offset in enumerate((1, -1, 2, -2)):
         copy = pltpu.make_async_remote_copy(
@@ -71,49 +124,11 @@
         copy.start()
         hot_copies.append(copy)
 
-    my_rows = x * 32 + core * 16
-
-    def raw_parts(block, chunk, x_at, core_at):
-        helper, owner, first = block
-        there = device(x_at, z + helper, core_at)
-        owner_index = device(x_at, z + owner, core_at)
-        columns = pl.ds(pl.multiple_of(owner_index * PIX + chunk * CPX, 128), CPX)
-        rows = pl.ds(pl.multiple_of(first + my_rows, 16), 16)
-        landing = pl.ds(pl.multiple_of(chunk * CPX, 128), CPX)
-        return src.at[:, columns], land.at[rows, landing], there
-
-    def send_raw(chunk, half):
-        away = (FAR[half],) + NEXT
-
-        def remote(block, x_at, core_at):
-            source, target, there = raw_parts(block, chunk, x_at, core_at)
-            pltpu.make_async_remote_copy(
-                src_ref=source, dst_ref=target, send_sem=raw_send.at[chunk], recv_sem=raw_recv.at[chunk],
-                device_id={"ifg": there}, device_id_type=MESH,
-            ).start()
-
-        for block in away:
-            remote(block, x, core)
-
-        def peer(step, carry):
-            for block in away + SAME:
-                remote(block, x + lax.div(step, 2), core + lax.rem(step, 2))
-            return carry
-
-        lax.fori_loop(1, 8, peer, 0)
-        for block in SAME:
-            source, target, _ = raw_parts(block, chunk, x, core)
-            pltpu.make_async_copy(source, target, raw_recv.at[chunk]).start()
-
-    def wait_raw(chunk, sem, rows):
-        view = land.at[pl.ds(0, rows), pl.ds(pl.multiple_of(chunk * CPX, 128), CPX)]
-        pltpu.make_async_copy(view, view, sem.at[chunk]).wait()
-
-    for chunk in range(LOOK):
-        send_raw(chunk, chunk // (NC // 2))
-
     date_at = lax.broadcasted_iota(jnp.int32, (256, 1024), 0)
-    placed = jnp.where(dates[...] < SEAM, dates[...], dates[...] + GAP)
+    dates = jnp.concatenate(
+        [date_pairs[:, at * 256 + row * 32 : at * 256 + row * 32 + 32] for row in range(8) for at in range(4)], axis=1
+    )
+    placed = jnp.where(dates < SEAM, dates, dates + GAP)
     signs = (date_at == placed[1:2, :]).astype(jnp.float32) - (date_at == placed[0:1, :]).astype(jnp.float32)
     design[...] = signs.astype(jnp.bfloat16)
     place = lax.broadcasted_iota(jnp.int32, (1, 1024), 1)
@@ -192,7 +207,7 @@
     def apply(weight, chunk, first, depth):
         data = land[first : first + depth, pl.ds(pl.multiple_of(chunk * CPX, 128), CPX)]
         both = jnp.dot(weight, data, preferred_element_type=jnp.float32)
-        return both[0:MP] + both[MP : 2 * MP]
+        return both[0:M] + both[MP : MP + M]
 
     def sum_copies(stage, chunk):
         copies = []
@@ -218,26 +233,30 @@
         for piece in range(CPX // 128):
             scale_out[stage, side, chunk, piece : piece + 1, :] = unit[:, piece * 128 : piece * 128 + 128]
 
-    def unpack(stage, side, chunk, rows):
+    def unpack(stage, side, chunk):
         unit = jnp.concatenate(
             [scale_in[stage, side, chunk, piece : piece + 1, :] for piece in range(CPX // 128)], axis=1
         )
-        return sums_in[stage, side, chunk, 0:rows, :].astype(jnp.int32).astype(jnp.float32) * unit
+        return sums_in[stage, side, chunk].astype(jnp.int32).astype(jnp.float32) * unit
+
+    def result_copy(chunk):
+        columns = pl.ds(pl.multiple_of(chunk * CPX, 128), CPX)
+        return pltpu.make_async_copy(total.at[chunk], out.at[:, columns], out_sem.at[chunk])
 
     def relay(chunk, run):
         for copy in sum_copies(0, chunk):
             copy.wait_recv()
         for side in range(2):
-            pack(apply(w_near[side, run], chunk, 128 + 128 * side, 128) + unpack(0, side, chunk, MP), 1, side, chunk)
+            pack(apply(w_near[side, run], chunk, 128 + 128 * side, 128) + unpack(0, side, chunk), 1, side, chunk)
         for copy in sum_copies(1, chunk):
             copy.start()
 
     def finish(chunk, run):
-        columns = pl.ds(pl.multiple_of(chunk * CPX, 128), CPX)
-        own = apply(w_own[run], chunk, 0, 128)[0:M]
+        own = apply(w_own[run], chunk, 0, 128)
         for copy in sum_copies(1, chunk):
             copy.wait_recv()
-        out[:, columns] = own + unpack(1, 0, chunk, M) + unpack(1, 1, chunk, M)
+        total[chunk] = own + unpack(1, 0, chunk) + unpack(1, 1, chunk)
+        result_copy(chunk).start()
 
     half_count = NC // 2
 
@@ -246,13 +265,6 @@
 
         def step(chunk, carry):
             wait_raw(chunk, raw_recv, 1024)
-            if half == 0:
-                ahead = chunk + LOOK
-
-                @pl.when(ahead < NC)
-                def _():
-                    send_raw(ahead, 1)
-
             pack(apply(w_left[half, :, 0:left_depth], chunk, 384, left_depth), 0, 0, chunk)
             pack(apply(w_right[half, :, 0 : 1024 - right_first], chunk, right_first, 1024 - right_first), 0, 1, chunk)
             for copy in sum_copies(0, chunk):
@@ -281,6 +293,7 @@
         wait_raw(chunk, raw_send, 944)
         for copy in sum_copies(0, chunk) + sum_copies(1, chunk):
             copy.wait_send()
+        result_copy(chunk).wait()
         return carry
 
     lax.fori_loop(0, NC, drain, 0)
@@ -289,20 +302,12 @@
 def local(phases, date_pairs, pair_counts, group_ids):
     rows = phases.shape[0]
     source = phases.reshape(rows, phases.shape[2])
-    dates = date_pairs.reshape(2, 4, 8, 32).transpose(0, 2, 1, 3).reshape(2, 1024)
-    groups = lax.dynamic_index_in_dim(group_ids, lax.axis_index("grp"), 0, keepdims=False)
-    run_groups = groups.reshape(2, 8)[:, 0]
-    picked = run_groups[:, None] == jnp.arange(16, dtype=jnp.int32)[None, :]
-    counts = jnp.sum(jnp.where(picked, pair_counts[None, :], 0), axis=1)
-    levels = jnp.array([128, 256, 512, 1024], jnp.int32)
-    hot = (levels[:, None] == counts[None, :]).astype(jnp.float32).reshape(8, 1)
-    hot = jnp.broadcast_to(hot, (8, 128))
     vmem = pl.BlockSpec(memory_space=pltpu.VMEM)
     solved = pl.pallas_call(
         body,
         out_shape=jax.ShapeDtypeStruct((M, PIX), jnp.float32),
-        in_specs=[pl.BlockSpec(memory_space=pl.ANY), vmem, vmem],
-        out_specs=vmem,
+        in_specs=[pl.BlockSpec(memory_space=pl.ANY), vmem, pl.BlockSpec(memory_space=pltpu.SMEM), vmem],
+        out_specs=pl.BlockSpec(memory_space=pl.ANY),
         scratch_shapes=[
             pltpu.VMEM((1024, PIX), jnp.bfloat16),
             pltpu.VMEM((8, 128, 128), jnp.float32),
@@ -313,10 +318,12 @@
             pltpu.VMEM((2, 2, 2 * MP, 128), jnp.bfloat16),
             pltpu.VMEM((2, 2 * MP, 384), jnp.bfloat16),
             pltpu.VMEM((2, 2 * MP, 384), jnp.bfloat16),
-            pltpu.VMEM((2, 2, NC, MP, CPX), jnp.int16),
-            pltpu.VMEM((2, 2, NC, MP, CPX), jnp.int16),
-            pltpu.VMEM((2, 2, NC, 8, 128), jnp.float32),
-            pltpu.VMEM((2, 2, NC, 8, 128), jnp.float32),
+            pltpu.VMEM((2, 2, NC, M, CPX), jnp.int16),
+            pltpu.VMEM((2, 2, NC, M, CPX), jnp.int16),
+            pltpu.VMEM((2, 2, NC, CPX // 128, 128), jnp.float32),
+            pltpu.VMEM((2, 2, NC, CPX // 128, 128), jnp.float32),
+            pltpu.VMEM((NC, M, CPX), jnp.float32),
+            pltpu.VMEM((8, 128), jnp.float32),
             pltpu.SemaphoreType.DMA((NC,)),
             pltpu.SemaphoreType.DMA((NC,)),
             pltpu.SemaphoreType.DMA((4,)),
@@ -325,11 +332,12 @@
             pltpu.SemaphoreType.DMA((2, 2, NC)),
             pltpu.SemaphoreType.DMA((2, 2, NC)),
             pltpu.SemaphoreType.DMA((2, 2, NC)),
+            pltpu.SemaphoreType.DMA((NC,)),
         ],
         compiler_params=pltpu.CompilerParams(
-            collective_id=0, has_side_effects=True, vmem_limit_bytes=60 * 1024 * 1024
+            collective_id=0, has_side_effects=True, vmem_limit_bytes=48 * 1024 * 1024
         ),
-    )(source, dates, hot)
+    )(source, date_pairs, pair_counts, group_ids)
     return solved[None, :, :]
 
 

time: 146 us -> 139 us (0.952)
  local copies, waits for them, and re-layouts: 7.09 us -> 3.74 us
  Pallas kernels: 137 us -> 135 us
  other arithmetic: 1.56 us -> 0 us
    reshape x4 -> x0, local copies, waits for them, and re-layouts: 1.56 us -> none  [the longest x3 1.48 us: local(): date_pairs.reshape(2, 4, 8, 32).transpose(0, 2, 1, 3).reshape(2, 1024)]
    unnamed x3 -> x7, local copies, waits for them, and re-layouts: 4.64 us -> 3.74 us
where the time goes in v3:
time: 139 us
  Pallas kernels  135 us (97%)
  local copies, waits for them, and re-layouts  3.74 us (3%)
    pallas_call x1, Pallas kernels, local(): pl.pallas_call(body, out_shape=jax.ShapeDtypeStruct((M, PIX), jnp.float32...  135 us
    unnamed x7, local copies, waits for them, and re-layouts  3.74 us

profile of v3, /device:TPU:1, one launch (start us, length us, event | category | flops | bytes accessed | tf_op | source)
XLA Modules:
  0.0 139.1 jit_solution(382462085140637117)
XLA Ops:
  0.0 0.0 copy-start
  0.0 0.7 copy-done
  0.7 0.0 copy-start.1
  0.7 0.7 copy-done.1
  1.4 0.0 copy-start.2
  1.4 0.7 copy-done.2
  2.0 135.3 %shard_map.46 = f32[200,4096]{1,0:T(8,128)S(1)} custom-call(bf16[16,262144]{1,0:T(8,128)(2,1)} %bitcast.3, s32[2,1024]{1,0:T(2,128)S(1)} %copy-done, s32[16]{0:T(128)S(1)} %copy-done.2, s32[4,16]{1,0:T(4,128)S(1)} %copy-done.1), custom_call_target="tpu_custom_call" | custom-call | tf_op jit(solution)/shard_map/pallas_call | solution.py:306
  137.4 1.7 %copy.6 = f32[1,200,4096]{2,1,0:T(8,128)} copy(f32[1,200,4096]{2,1,0:T(8,128)S(1)} %bitcast.2) | data formatting | bytes 6553600
Async XLA Ops:
  0.0 0.7 copy-start
  0.7 0.7 copy-start.1
  1.4 0.7 copy-start.2
